TPU v7x, 128 devices: a whole 4x4x4 slice. The times are simulated.
128 devices in a mesh: dp: 64 (over z, y, x_hi, core), feat: 2 (over x_lo).
Axes of the slice: x: 4 (x_hi: 2, x_lo: 2; x = x_hi * 2 + x_lo), y: 4, z: 4, core: 2. Of those that a mesh axis runs over, the one named last changes fastest.
Arguments:
- embeddings: bfloat16 [131072, 1024], P('dp', 'feat')
- assignments: int32 [131072], P('dp'), may hold values from 0 to 511, as said below
- order_index: int32 [131072], P('dp'), may hold values from 0 to 131071, each once
- cluster_blocks: int32 [512], replicated, may hold values from 1 to 4, as said below
Outputs:
- centroids: bfloat16 [512, 1024], P('dp', 'feat')
- centroid_sim: float32 [131072], P('dp')
- earlier_max: float32 [131072], P('dp')
Inputs may be any that keep to these rules, and one draw needn't show every extreme that they name: `assignments`: every cluster holds at least one row. The rows of one index of dp name one cluster at most 8 times, and on every index some cluster exactly 8 times. `cluster_blocks`: the number of rows of the cluster divided by 128, rounded up; some cluster has 512 rows.
All inputs are finite; a program needn't handle non-finite values.
Results may differ from a plain program's by a relative error of at most 0.0012.
Values may be sent and summed in bfloat16 or wider, within the bound.
A program may use at most 64 MiB of HBM per device.

v0:
```python
from functools import partial

import jax
import jax.numpy as jnp
from jax import lax
from jax.sharding import PartitionSpec as P

epsilon = 1e-06
block_rows = 128


def masked_best(unit_rows, row_order, used_rows):
    leading = unit_rows[:used_rows]
    key_order = row_order[:used_rows]
    similar = jnp.dot(leading, leading.T, preferred_element_type=jnp.float32)
    earlier = (key_order[None, :] < key_order[:, None]) & (key_order[None, :] >= 0)
    best_match = jnp.max(jnp.where(earlier, similar, jnp.float32(-1.0)), axis=1)
    filler = jnp.full((unit_rows.shape[0] - used_rows,), -1.0, jnp.float32)
    return jnp.concatenate([best_match, filler])


def cluster_best(unit_rows, row_order, blocks_used):
    capacity = unit_rows.shape[0]
    branches = [
        partial(masked_best, used_rows=(level + 1) * block_rows)
        for level in range(capacity // block_rows)
    ]
    return lax.switch(blocks_used - 1, branches, unit_rows, row_order)


def compact(got_rows, got_order):
    n_sources, n_clusters, per_source, width = got_rows.shape
    capacity = n_sources * per_source
    filled = got_order >= 0
    source_counts = jnp.sum(filled, axis=2)
    offsets = jnp.cumsum(source_counts, axis=0) - source_counts
    position = offsets[:, :, None] + jnp.arange(per_source, dtype=jnp.int32)[None, None, :]
    target = jnp.where(filled, position, -1).transpose(1, 0, 2).reshape(n_clusters, capacity)
    rows_by_cluster = got_rows.transpose(1, 0, 2, 3).reshape(n_clusters, capacity, width)
    order_by_cluster = got_order.transpose(1, 0, 2).reshape(n_clusters, capacity)
    placing = jnp.arange(capacity, dtype=jnp.int32)[None, :, None] == target[:, None, :]
    packed = jnp.einsum(
        "cdu,cuw->cdw",
        placing.astype(jnp.bfloat16),
        rows_by_cluster,
        preferred_element_type=jnp.float32,
    ).astype(jnp.bfloat16)
    packed_order = jnp.max(jnp.where(placing, order_by_cluster[:, None, :], -1), axis=2).astype(
        jnp.int32
    )
    return (packed, packed_order, placing)


def unpack(results, placing, n_sources, per_source):
    n_clusters = results.shape[0]
    back = jnp.sum(jnp.where(placing, results[:, :, None], jnp.float32(0.0)), axis=1)
    return back.reshape(n_clusters, n_sources, per_source).transpose(1, 0, 2)


def body(embeddings, assignments, order_index, cluster_blocks):
    n_owners = lax.axis_size("dp")
    clusters = cluster_blocks.shape[0]
    cl_local = clusters // n_owners
    rows_here = assignments.shape[0]
    local_width = embeddings.shape[1]
    per_source = 2 * rows_here // clusters
    capacity = n_owners * per_source
    n_slots = clusters * per_source
    my_owner = lax.axis_index("dp")
    row_block = min(512, rows_here)
    n_row_blocks = rows_here // row_block
    member = jnp.arange(clusters, dtype=jnp.int32)[:, None] == assignments[None, :]
    onehot = member.astype(jnp.bfloat16)
    partial_sums = jnp.dot(onehot, embeddings, preferred_element_type=jnp.float32)
    local_counts = jnp.sum(member, axis=1)
    partial_counts = local_counts.astype(jnp.float32)
    total_sums, total_counts = lax.psum((partial_sums, partial_counts), "dp")
    averages = total_sums / total_counts[:, None]
    centre_norms = lax.psum(jnp.sum(averages * averages, axis=1), "feat")
    centroids = (averages / jnp.sqrt(centre_norms + epsilon)[:, None]).astype(jnp.bfloat16)
    own_centroids = lax.dynamic_slice_in_dim(centroids, my_owner * cl_local, cl_local, 0)
    values = embeddings.astype(jnp.float32)
    row_centres = lax.dot_general(
        onehot, centroids, (((0,), (0,)), ((), ())), preferred_element_type=jnp.float32
    )
    square_part = jnp.sum(values * values, axis=1)
    product_part = jnp.sum(values * row_centres, axis=1)
    squares, products = lax.psum((square_part, product_part), "feat")
    lengths = jnp.sqrt(squares + epsilon)
    centroid_sim = products / lengths
    normed = (values / lengths[:, None]).astype(jnp.bfloat16)
    member_blocks = member.reshape(clusters, n_row_blocks, row_block)
    before = (jnp.arange(row_block)[:, None] < jnp.arange(row_block)[None, :]).astype(jnp.bfloat16)
    within = jnp.einsum(
        "kbr,rs->kbs",
        member_blocks.astype(jnp.bfloat16),
        before,
        preferred_element_type=jnp.float32,
    )
    block_totals = jnp.sum(member_blocks, axis=2)
    block_offsets = (jnp.cumsum(block_totals, axis=1) - block_totals).astype(jnp.float32)
    rank_table = (within + block_offsets[:, :, None]).reshape(clusters, rows_here)
    row_rank = jnp.sum(jnp.where(member, rank_table, jnp.float32(0.0)), axis=0).astype(jnp.int32)
    send_slot = assignments * per_source + row_rank
    slot_ids = jnp.arange(n_slots, dtype=jnp.int32)

    def place_block(block_index, carry):
        rows_acc, order_acc = carry
        start = block_index * row_block
        slot_piece = lax.dynamic_slice_in_dim(send_slot, start, row_block, 0)
        rows_piece = lax.dynamic_slice_in_dim(normed, start, row_block, 0)
        order_piece = lax.dynamic_slice_in_dim(order_index, start, row_block, 0)
        hits = slot_ids[:, None] == slot_piece[None, :]
        rows_acc = rows_acc + jnp.dot(
            hits.astype(jnp.bfloat16), rows_piece, preferred_element_type=jnp.float32
        )
        order_acc = jnp.maximum(
            order_acc, jnp.max(jnp.where(hits, order_piece[None, :], -1), axis=1)
        )
        return (rows_acc, order_acc)

    placed_rows, send_order = lax.fori_loop(
        0,
        n_row_blocks,
        place_block,
        (jnp.zeros((n_slots, local_width), jnp.float32), jnp.full((n_slots,), -1, jnp.int32)),
    )
    send_rows = placed_rows.astype(jnp.bfloat16)
    my_blocks = lax.dynamic_slice_in_dim(cluster_blocks, my_owner * cl_local, cl_local, 0)
    got_rows, got_order = (
        lax.all_to_all(
            send_rows.reshape(n_owners, cl_local * per_source, local_width),
            "dp",
            split_axis=0,
            concat_axis=0,
            tiled=True,
        ),
        lax.all_to_all(
            send_order.reshape(n_owners, cl_local * per_source),
            "dp",
            split_axis=0,
            concat_axis=0,
            tiled=True,
        ),
    )
    got_rows = got_rows.reshape(n_owners, cl_local, per_source, local_width)
    got_order = got_order.reshape(n_owners, cl_local, per_source)
    packed, packed_order, placing = compact(got_rows, got_order)

    def visit(cluster_index, results):
        slice_rows = lax.dynamic_index_in_dim(packed, cluster_index, 0, keepdims=False)
        full_rows = lax.all_gather(slice_rows, "feat", axis=1, tiled=True)
        key_order = lax.dynamic_index_in_dim(packed_order, cluster_index, 0, keepdims=False)
        best_match = cluster_best(full_rows, key_order, my_blocks[cluster_index])
        return lax.dynamic_update_index_in_dim(results, best_match, cluster_index, 0)

    results = lax.fori_loop(0, cl_local, visit, jnp.zeros((cl_local, capacity), jnp.float32))
    answer = unpack(results, placing, n_owners, per_source).reshape(n_owners, cl_local * per_source)
    returned = lax.all_to_all(answer, "dp", split_axis=0, concat_axis=0, tiled=True)
    returned_flat = returned.reshape(n_slots)

    def read_block(block_index):
        slot_piece = lax.dynamic_slice_in_dim(send_slot, block_index * row_block, row_block, 0)
        hits = slot_ids[:, None] == slot_piece[None, :]
        return jnp.sum(jnp.where(hits, returned_flat[:, None], jnp.float32(0.0)), axis=0)

    earlier_max = lax.map(read_block, jnp.arange(n_row_blocks, dtype=jnp.int32)).reshape(rows_here)
    return (own_centroids, centroid_sim, earlier_max)


def solution(mesh):
    return jax.shard_map(
        body,
        mesh=mesh,
        in_specs=(P("dp", "feat"), P("dp"), P("dp"), P()),
        out_specs=(P("dp", "feat"), P("dp"), P("dp")),
        check_vma=False,
    )
```

profile of v0, /device:TPU:1, one launch (start us, length us, event | category | flops | bytes accessed | tf_op | source)
XLA Modules:
  0.0 1076.3 jit_solution(17446821728858519942)
XLA Ops:
  7.2 3.8 fusion.26
  12.2 2.9 copy.39
  15.2 1.7 select_reduce_fusion.3
  16.9 165.0 %psum.36 = f32[512]{0:T(512)S(1)} all-reduce(f32[512]{0:T(512)S(1)} %convert_element_type.51), channel_id=1, replica_groups=mesh['dp'=64,'feat'=2] {'dp'}, use_global_device_ids=true, to_apply=%region_2.0 | all-reduce | flops 512 | bytes 4096 | tf_op jit(solution)/shard_map/psum | solution.py:77
  182.3 467.5 %all-reduce.6.cloned.1.call-done = f32[512,512]{1,0:T(8,128)} async-done(((f32[512,512]{1,0:T(8,128)}), f32[512,512]{1,0:T(8,128)}) %all-reduce.6.cloned.1.call-update) | async-done | bytes 1048592 | tf_op jit(solution)/shard_map/psum | solution.py:77
  649.9 1.5 multiply_reduce_fusion
  651.4 3.8 psum.37
  655.2 1.4 divide_convert_fusion
  656.5 1.5 fusion.18
  658.0 5.2 all-reduce.3
  663.8 1.9 fusion.20
  665.7 43.8 %while.44 = (s32[]{:T(128)}, f32[4096,512]{1,0:T(8,128)}, s32[4096]{0:T(1024)S(1)}, s32[2048]{0:T(1024)S(1)}, bf16[2048,512]{0,1:T(8,128)(2,1)}, /*index=5*/s32[...) while((s32[]{:T(128)}, f32[4096,512]{1,0:T(8,128)}, s32[4096]{0:T(1024)S(1)}, ...), condition=%wide.region_14.15_spmd.clone, body=%wide.region_12.14_spmd.clone.sunk | while | flops 2160070656 | bytes 17381552 | solution.py:122
  666.6 1.2 fusion.44
  667.8 7.0 select_add_fusion.2
  675.6 1.2 fusion.44
  676.9 9.5 select_add_fusion.2
  687.2 1.2 fusion.44
  688.5 9.5 select_add_fusion.2
  698.8 1.2 fusion.44
  700.1 9.5 select_add_fusion.2
  710.3 12.7 %all-to-all-start = ((s32[64,1,64]{2,1,0:T(1,128)}), s32[64,1,64]{2,1,0:T(1,128)S(1)}, u32[]{:S(2)}, u32[]{:S(2)}) async-start(s32[64,1,64]{2,1,0:T(1,128)} %bitcast.10), calls=%async_computation | async-start | bytes 65536 | tf_op jit(solution)/shard_map/all_to_all | solution.py:138
  723.0 5.9 convert_element_type.60
  728.9 3.3 all-to-all-done
  732.2 7.2 all-to-all-start.1
  741.2 1.4 select_reduce_fusion.2
  742.6 50.1 %all-to-all-done.1 = bf16[64,64,512]{2,1,0:T(8,128)(2,1)} async-done(((bf16[64,64,512]{2,1,0:T(8,128)(2,1)}), bf16[64,64,512]{2,1,0:T(8,128)(2,1)}, u32[]{:S(2)}, u32[]{:S(2)}) %all-to-all-start.1) | async-done | bytes 4194336 | tf_op jit(solution)/shard_map/all_to_all | solution.py:131
  792.7 6.5 fusion.27
  799.1 236.7 %while.43 = (s32[]{:T(128)}, f32[8,512]{1,0:T(8,128)S(1)}, s32[8]{0:T(128)S(1)}, bf16[8,512,512]{2,1,0:T(8,128)(2,1)}, s32[8,512]{1,0:T(8,128)S(1)}, /*index=5*/...) while((s32[]{:T(128)}, f32[8,512]{1,0:T(8,128)S(1)}, s32[8]{0:T(128)S(1)}, ...), condition=%wide.region_27.28_spmd, body=%wide.region_18.27_spmd.sunk | while | flops 537919488 | bytes 6831409 | solution.py:157
  799.1 1.9 constant_dynamic-slice_fusion.5
  802.2 26.4 %all-gather.5.cloned.1.call-done = bf16[1,512,1024]{2,1,0:T(8,128)(2,1)} async-done(((bf16[1,512,512]{2,1,0:T(8,128)(2,1)}), bf16[1,512,1024]{2,1,0:T(8,128)(2,1)}) %all-gather.5.cloned.1.call-update) | async-done | bytes 1048592 | tf_op jit(solution)/shard_map/while/body/eval_jaxpr/all_gather | solution.py:152
  828.6 2.0 conditional.2
  828.6 2.0 fusion.15
  830.7 1.9 constant_dynamic-slice_fusion.5
  833.8 24.3 %all-gather.5.cloned.1.call-done = bf16[1,512,1024]{2,1,0:T(8,128)(2,1)} async-done(((bf16[1,512,512]{2,1,0:T(8,128)(2,1)}), bf16[1,512,1024]{2,1,0:T(8,128)(2,1)}) %all-gather.5.cloned.1.call-update) | async-done | bytes 1048592 | tf_op jit(solution)/shard_map/while/body/eval_jaxpr/all_gather | solution.py:152
  858.1 1.3 conditional.2
  858.1 1.3 fusion.4
  859.5 1.9 constant_dynamic-slice_fusion.5
  862.6 24.8 %all-gather.5.cloned.1.call-done = bf16[1,512,1024]{2,1,0:T(8,128)(2,1)} async-done(((bf16[1,512,512]{2,1,0:T(8,128)(2,1)}), bf16[1,512,1024]{2,1,0:T(8,128)(2,1)}) %all-gather.5.cloned.1.call-update) | async-done | bytes 1048592 | tf_op jit(solution)/shard_map/while/body/eval_jaxpr/all_gather | solution.py:152
  887.4 2.0 conditional.2
  887.5 2.0 fusion.15
  889.6 1.9 constant_dynamic-slice_fusion.5
  892.7 24.0 %all-gather.5.cloned.1.call-done = bf16[1,512,1024]{2,1,0:T(8,128)(2,1)} async-done(((bf16[1,512,512]{2,1,0:T(8,128)(2,1)}), bf16[1,512,1024]{2,1,0:T(8,128)(2,1)}) %all-gather.5.cloned.1.call-update) | async-done | bytes 1048592 | tf_op jit(solution)/shard_map/while/body/eval_jaxpr/all_gather | solution.py:152
  916.7 2.3 conditional.2
  916.7 2.3 fusion.8
  919.1 1.9 constant_dynamic-slice_fusion.5
  922.2 23.7 %all-gather.5.cloned.1.call-done = bf16[1,512,1024]{2,1,0:T(8,128)(2,1)} async-done(((bf16[1,512,512]{2,1,0:T(8,128)(2,1)}), bf16[1,512,1024]{2,1,0:T(8,128)(2,1)}) %all-gather.5.cloned.1.call-update) | async-done | bytes 1048592 | tf_op jit(solution)/shard_map/while/body/eval_jaxpr/all_gather | solution.py:152
  945.9 1.3 conditional.2
  945.9 1.3 fusion.4
  947.3 1.9 constant_dynamic-slice_fusion.5
  950.4 25.0 %all-gather.5.cloned.1.call-done = bf16[1,512,1024]{2,1,0:T(8,128)(2,1)} async-done(((bf16[1,512,512]{2,1,0:T(8,128)(2,1)}), bf16[1,512,1024]{2,1,0:T(8,128)(2,1)}) %all-gather.5.cloned.1.call-update) | async-done | bytes 1048592 | tf_op jit(solution)/shard_map/while/body/eval_jaxpr/all_gather | solution.py:152
  975.4 2.0 conditional.2
  975.4 2.0 fusion.15
  977.6 1.9 constant_dynamic-slice_fusion.5
  980.6 24.3 %all-gather.5.cloned.1.call-done = bf16[1,512,1024]{2,1,0:T(8,128)(2,1)} async-done(((bf16[1,512,512]{2,1,0:T(8,128)(2,1)}), bf16[1,512,1024]{2,1,0:T(8,128)(2,1)}) %all-gather.5.cloned.1.call-update) | async-done | bytes 1048592 | tf_op jit(solution)/shard_map/while/body/eval_jaxpr/all_gather | solution.py:152
  1004.9 1.3 conditional.2
  1005.0 1.3 fusion.4
  1006.4 1.9 constant_dynamic-slice_fusion.5
  1009.5 25.0 %all-gather.5.cloned.1.call-done = bf16[1,512,1024]{2,1,0:T(8,128)(2,1)} async-done(((bf16[1,512,512]{2,1,0:T(8,128)(2,1)}), bf16[1,512,1024]{2,1,0:T(8,128)(2,1)}) %all-gather.5.cloned.1.call-update) | async-done | bytes 1048592 | tf_op jit(solution)/shard_map/while/body/eval_jaxpr/all_gather | solution.py:152
  1034.5 1.3 conditional.2
  1034.5 1.3 fusion.4
  1035.9 1.3 select_reduce_fusion.1
  1038.2 11.1 %all-to-all-start.2 = ((f32[64,1,64]{2,1,0:T(1,128)}), f32[64,1,64]{2,1,0:T(1,128)S(1)}, u32[]{:S(2)}, u32[]{:S(2)}) async-start(f32[64,1,64]{2,1,0:T(1,128)} %copy.50), calls=%async_computation.2 | async-start | bytes 65536 | tf_op jit(solution)/shard_map/all_to_all | solution.py:159
  1049.8 8.6 all-to-all-done.2
  1059.1 10.1 while.45
  (121 shorter events, 24.0 us)
Async XLA Ops:
  7.2 3.9 copy-start.1
  7.2 642.7 %all-reduce.6.cloned.1.call-start = ((), (), s32[]{:S(2)}) async-start(), calls=%async_computation.3 | async-start | bytes 2097152 | tf_op jit(solution)/shard_map/psum | solution.py:77
  710.3 22.0 %all-to-all-start = ((s32[64,1,64]{2,1,0:T(1,128)}), s32[64,1,64]{2,1,0:T(1,128)S(1)}, u32[]{:S(2)}, u32[]{:S(2)}) async-start(s32[64,1,64]{2,1,0:T(1,128)} %bitcast.10), calls=%async_computation | async-start | bytes 65536 | tf_op jit(solution)/shard_map/all_to_all | solution.py:138
  732.2 60.4 %all-to-all-start.1 = ((bf16[64,64,512]{2,1,0:T(8,128)(2,1)}), bf16[64,64,512]{2,1,0:T(8,128)(2,1)}, u32[]{:S(2)}, u32[]{:S(2)}) async-start(bf16[64,64,512]{2,1,0:T(8,128)(2,1)} %bitcast.58), calls=%async_computation.1 | async-start | bytes 8388608 | tf_op jit(solution)/shard_map/all_to_all | solution.py:131
  799.1 29.4 %all-gather.5.cloned.1.call-start = ((), (), s32[]{:S(2)}) async-start(), calls=%async_computation.4 | async-start | bytes 1572864 | tf_op jit(solution)/shard_map/while/body/eval_jaxpr/all_gather | solution.py:152
  830.7 27.4 %all-gather.5.cloned.1.call-start = ((), (), s32[]{:S(2)}) async-start(), calls=%async_computation.4 | async-start | bytes 1572864 | tf_op jit(solution)/shard_map/while/body/eval_jaxpr/all_gather | solution.py:152
  859.5 27.9 %all-gather.5.cloned.1.call-start = ((), (), s32[]{:S(2)}) async-start(), calls=%async_computation.4 | async-start | bytes 1572864 | tf_op jit(solution)/shard_map/while/body/eval_jaxpr/all_gather | solution.py:152
  889.5 27.1 %all-gather.5.cloned.1.call-start = ((), (), s32[]{:S(2)}) async-start(), calls=%async_computation.4 | async-start | bytes 1572864 | tf_op jit(solution)/shard_map/while/body/eval_jaxpr/all_gather | solution.py:152
  919.1 26.8 %all-gather.5.cloned.1.call-start = ((), (), s32[]{:S(2)}) async-start(), calls=%async_computation.4 | async-start | bytes 1572864 | tf_op jit(solution)/shard_map/while/body/eval_jaxpr/all_gather | solution.py:152
  947.3 28.1 %all-gather.5.cloned.1.call-start = ((), (), s32[]{:S(2)}) async-start(), calls=%async_computation.4 | async-start | bytes 1572864 | tf_op jit(solution)/shard_map/while/body/eval_jaxpr/all_gather | solution.py:152
  977.5 27.4 %all-gather.5.cloned.1.call-start = ((), (), s32[]{:S(2)}) async-start(), calls=%async_computation.4 | async-start | bytes 1572864 | tf_op jit(solution)/shard_map/while/body/eval_jaxpr/all_gather | solution.py:152
  1006.3 28.1 %all-gather.5.cloned.1.call-start = ((), (), s32[]{:S(2)}) async-start(), calls=%async_computation.4 | async-start | bytes 1572864 | tf_op jit(solution)/shard_map/while/body/eval_jaxpr/all_gather | solution.py:152
  1038.2 20.3 %all-to-all-start.2 = ((f32[64,1,64]{2,1,0:T(1,128)}), f32[64,1,64]{2,1,0:T(1,128)S(1)}, u32[]{:S(2)}, u32[]{:S(2)}) async-start(f32[64,1,64]{2,1,0:T(1,128)} %copy.50), calls=%async_computation.2 | async-start | bytes 65536 | tf_op jit(solution)/shard_map/all_to_all | solution.py:159
  1058.5 0.6 copy-start
Sparse Core Ops, SparseCore 0:
  11.2 638.6 all-reduce.5
  801.7 26.8 all-gather.4
  833.3 24.7 all-gather.4
  861.8 25.6 all-gather.4
  891.8 24.7 all-gather.4
  921.4 24.4 all-gather.4
  949.9 25.4 all-gather.4
  980.1 24.7 all-gather.4
  1008.9 25.4 all-gather.4
where the time goes:
time: 1080 us
  waiting for transfers between devices  727 us (67%)
  blocking collectives  174 us (16%)
  matrix products  62.4 us (6%)
  local copies, waits for them, and re-layouts  34.7 us (3%)
  starting transfers between devices  31.3 us (3%)
  other arithmetic  25.2 us (2%)
  between operations  13.9 us (1%)
    psum x1, waiting for transfers between devices, body(): total_sums, total_counts = lax.psum((partial_sums, partial_counts), 'dp')  468 us
    all_gather x8, waiting for transfers between devices, visit(): full_rows = lax.all_gather(slice_rows, 'feat', axis=1, tiled=True)  197 us
    psum x1, blocking collectives, body(): total_sums, total_counts = lax.psum((partial_sums, partial_counts), 'dp')  165 us
    all_to_all x1, waiting for transfers between devices, body(): lax.all_to_all(send_rows.reshape(n_owners, cl_local * per_source, local_w...  50.1 us
    dot_general x4, matrix products, place_block(): jnp.dot(hits.astype(jnp.bfloat16), rows_piece, preferred_element_type=jnp...  35.5 us
  transfers between devices with their start and end apart: 12, of which 12 were waited for; matrix products, arithmetic and copies ran while one was open for 2% of the time, Pallas kernels for 0%

commit v1 on v0

v1 whole, which is shorter than its diff:
```python
from functools import partial

import jax
import jax.numpy as jnp
from jax import lax
from jax.experimental import pallas as pl
from jax.experimental.pallas import tpu as pltpu
from jax.sharding import PartitionSpec as P

epsilon = 1e-06
MESH = pl.DeviceIdType.MESH
NT = (((1,), (1,)), ((), ()))
TN = (((0,), (0,)), ((), ()))

LOCAL = 4
SLOTS = 8
SOURCES = 64
DEVICES = 128
CHUNK = 32
BIG = float(2**20)


def iota(shape, axis):
    return lax.broadcasted_iota(jnp.int32, shape, axis)


def position():
    dp = lax.axis_index("dp")
    feat = lax.axis_index("feat")
    return dp, feat, (dp // 16, (dp // 4) % 4, (dp // 2) % 2 * 2 + feat, dp % 2)


def shifted(place, k):
    z, y, x, core = place
    tz = (z + k % 4) % 4
    ty = (y + (k // 4) % 4) % 4
    tx = (x + (k // 16) % 4) % 4
    tc = (core + k // 64) % 2
    return ((tz * 4 + ty) * 2 + tx // 2) * 2 + tc, tx % 2


def shifted_owner(place, k):
    z, y, x, core = place
    tz = (z + (k & 3)) & 3
    ty = (y + ((k >> 2) & 3)) & 3
    tx = (x + ((k >> 4) & 3)) & 3
    tc = (core + (k >> 6)) & 1
    return (tz << 5) + (ty << 3) + ((tx >> 1) << 2) + (tc << 1) + (tx & 1)


def onehot(condition):
    return jnp.where(condition, 1.0, 0.0).astype(jnp.bfloat16)


def thirds(values):
    high = values.astype(jnp.bfloat16)
    rest = values - high.astype(jnp.float32)
    middle = rest.astype(jnp.bfloat16)
    low = (rest - middle.astype(jnp.float32)).astype(jnp.bfloat16)
    return high, middle, low


def f32_dot(a, b, dims):
    return lax.dot_general(a, b, dims, preferred_element_type=jnp.float32)


def kernel(
    rows_hbm,
    assign_ref,
    order_ref,
    cent_ref,
    sim_ref,
    best_ref,
    rows,
    slot_of_row,
    hits_owner,
    send,
    recv,
    meta_send,
    meta_recv,
    key_cols,
    key_rows,
    cent_mine,
    cent_other,
    back_send,
    back_recv,
    load_sem,
    send_sem,
    recv_sem,
    meta_send_sem,
    meta_recv_sem,
    cent_send_sem,
    cent_recv_sem,
    back_send_sem,
    back_recv_sem,
):
    dp, feat, place = position()
    n_rows = rows.shape[0]
    width = rows.shape[1]
    members = SOURCES * SLOTS
    load = pltpu.make_async_copy(rows_hbm, rows, load_sem)
    load.start()

    barrier = pltpu.get_barrier_semaphore()

    def greet(k, carry):
        tdp, tfeat = shifted(place, k)
        pl.semaphore_signal(barrier, inc=1, device_id=(tdp, tfeat), device_id_type=MESH)
        return carry

    lax.fori_loop(1, DEVICES, greet, 0)

    part = 256
    n_clusters = DEVICES * LOCAL
    before = onehot(iota((part, part), 0) < iota((part, part), 1))
    ones = jnp.ones((part, part), jnp.bfloat16)

    counted = jnp.zeros((n_clusters, part), jnp.float32)
    for block in range(n_rows // part):
        piece = assign_ref[:, block * part : (block + 1) * part]
        member = iota((n_clusters, part), 0) == piece
        member_b = onehot(member)
        ahead = jnp.dot(member_b, before, preferred_element_type=jnp.float32) + counted
        rank = jnp.sum(jnp.where(member, ahead, 0.0), axis=0, keepdims=True)
        slot_of_row[:, block * part : (block + 1) * part] = piece * SLOTS + rank.astype(jnp.int32)
        if block + 1 < n_rows // part:
            counted = counted + jnp.dot(member_b, ones, preferred_element_type=jnp.float32)

    slots = slot_of_row[...]
    own_slots = LOCAL * SLOTS
    hits_owner[...] = onehot(iota((DEVICES, n_rows), 0) == (slots >> 5))
    orders = order_ref[...]
    line = iota((DEVICES, n_rows), 0)
    kind = line >> 5
    digit = jnp.where(
        kind == 0,
        orders >> 14,
        jnp.where(kind == 1, (orders >> 7) & 127, jnp.where(kind == 2, orders & 127, 1)),
    )
    digits = jnp.where((line & 31) == (slots & 31), digit, 0).astype(jnp.float32)
    meta = f32_dot(hits_owner[...], digits.astype(jnp.bfloat16), NT)
    meta_send[:, 0, :] = meta

    load.wait()
    pl.semaphore_wait(barrier, DEVICES - 1)

    def meta_out(k, carry):
        tdp, tfeat = shifted(place, k)

        @pl.when(tfeat == feat)
        def _():
            pltpu.make_async_remote_copy(
                meta_send.at[tdp * 2 + feat],
                meta_recv.at[dp],
                meta_send_sem,
                meta_recv_sem,
                device_id=(tdp, feat),
                device_id_type=MESH,
            ).start()

        return carry

    lax.fori_loop(1, DEVICES, meta_out, 0)
    pltpu.make_async_copy(meta_send.at[dp * 2 + feat], meta_recv.at[dp], meta_recv_sem).start()

    n_chunks = DEVICES // CHUNK

    def pack(step, carry):
        local = step // n_chunks
        chunk = step % n_chunks
        q = iota((CHUNK * SLOTS, 1), 0)
        owner = shifted_owner(place, chunk * CHUNK + (q >> 3))
        wanted = owner * own_slots + local * SLOTS + (q & 7)
        hits = onehot(wanted == slot_of_row[...])
        packed = jnp.dot(hits, rows[...], preferred_element_type=jnp.float32)
        send[local, pl.ds(chunk * CHUNK, CHUNK)] = packed.reshape(CHUNK, SLOTS, width).astype(
            jnp.bfloat16
        )

        def ship(i, carry):
            k = chunk * CHUNK + i
            tdp, tfeat = shifted(place, k)
            pltpu.make_async_remote_copy(
                send.at[local, k],
                recv.at[local, feat, dp],
                send_sem.at[local],
                recv_sem.at[local],
                device_id=(tdp, tfeat),
                device_id_type=MESH,
            ).start()
            return carry

        @pl.when(chunk == 0)
        def _():
            pltpu.make_async_copy(
                send.at[local, 0], recv.at[local, feat, dp], recv_sem.at[local]
            ).start()
            lax.fori_loop(1, CHUNK, ship, 0)

        @pl.when(chunk > 0)
        def _():
            lax.fori_loop(0, CHUNK, ship, 0)

        return carry

    lax.fori_loop(0, LOCAL * n_chunks, pack, 0)

    pltpu.make_async_copy(meta_recv, meta_recv, meta_recv_sem).wait()
    meta_in = meta_recv[:, 0, :].astype(jnp.bfloat16)
    of_source = onehot(iota((SOURCES, members), 0) == (iota((SOURCES, members), 1) >> 3))

    def scale_of(index):
        kind = index >> 5
        return jnp.where(
            kind == 0, 16384.0, jnp.where(kind == 1, 128.0, jnp.where(kind == 2, 1.0, -BIG))
        )

    across = f32_dot(meta_in, of_source, TN) * scale_of(iota((DEVICES, members), 0))
    down = f32_dot(of_source, meta_in, TN) * scale_of(iota((members, DEVICES), 1))
    filled_counts = []
    for local in range(LOCAL):
        pick = (iota((DEVICES, members), 0) & 31) == local * SLOTS + (iota((DEVICES, members), 1) & 7)
        key_rows[local] = BIG + jnp.sum(jnp.where(pick, across, 0.0), axis=0, keepdims=True)
        pick = (iota((members, DEVICES), 1) & 31) == local * SLOTS + (iota((members, DEVICES), 0) & 7)
        key_cols[local] = BIG + jnp.sum(jnp.where(pick, down, 0.0), axis=1, keepdims=True)

    lane = iota((members, DEVICES), 1)
    slot_of_member = iota((members, DEVICES), 0) & 7
    back = jnp.zeros((SOURCES, DEVICES), jnp.float32)
    for local in range(LOCAL):
        pltpu.make_async_copy(recv.at[local], recv.at[local], recv_sem.at[local]).wait()
        values = jnp.concatenate(
            [recv[local, h].astype(jnp.float32).reshape(members, width) for h in range(2)], axis=1
        )
        order_row = key_rows[local]
        order_col = key_cols[local]
        count = jnp.sum(jnp.where(order_row < BIG, 1.0, 0.0), axis=1, keepdims=True)
        squares = jnp.sum(values * values, axis=1, keepdims=True)
        lengths = jnp.sqrt(squares + epsilon)
        averages = jnp.sum(values, axis=0, keepdims=True) / count
        norm = jnp.sum(averages * averages, axis=1, keepdims=True)
        centroid = (averages / jnp.sqrt(norm + epsilon)).astype(jnp.bfloat16).astype(jnp.float32)
        for h in range(2):
            half = centroid[:, h * width : (h + 1) * width]
            cent_mine[h, local : local + 1] = half
            cent_mine[h, local + LOCAL : local + LOCAL + 1] = half
        products = jnp.sum(values * centroid, axis=1, keepdims=True)
        inverse = 1.0 / lengths
        sim = products * inverse
        unit = (values * inverse).astype(jnp.bfloat16)
        similar = f32_dot(unit, unit, NT)
        best = jnp.max(jnp.where(order_col < order_row, similar, -1.0), axis=0, keepdims=True)
        best_of_source = jnp.where(
            iota((SOURCES, members), 0) == (iota((SOURCES, members), 1) >> 3), best, 0.0
        )
        to_lane = onehot(lane == local * SLOTS + slot_of_member)
        sim_lanes = jnp.where(lane == (LOCAL + local) * SLOTS + slot_of_member, sim, 0.0)
        for piece in thirds(best_of_source):
            back = back + jnp.dot(piece, to_lane, preferred_element_type=jnp.float32)
        for piece in thirds(sim_lanes):
            back = back + jnp.dot(of_source, piece, preferred_element_type=jnp.float32)

    back_send[:, 0, :] = back
    swap = pltpu.make_async_remote_copy(
        cent_mine.at[1 - feat],
        cent_other,
        cent_send_sem,
        cent_recv_sem,
        device_id=(dp, 1 - feat),
        device_id_type=MESH,
    )

    def back_out(k, carry):
        tdp, tfeat = shifted(place, k)
        pltpu.make_async_remote_copy(
            back_send.at[tdp],
            back_recv.at[dp * 2 + feat],
            back_send_sem,
            back_recv_sem,
            device_id=(tdp, tfeat),
            device_id_type=MESH,
        ).start()
        return carry

    lax.fori_loop(1, DEVICES, back_out, 0)
    pltpu.make_async_copy(back_send.at[dp], back_recv.at[dp * 2 + feat], back_recv_sem).start()
    swap.start()

    pltpu.make_async_copy(back_recv, back_recv, back_recv_sem).wait()
    table = back_recv[:, 0, :]
    hits = hits_owner[...]
    found = jnp.zeros((DEVICES, n_rows), jnp.float32)
    for piece in thirds(table):
        found = found + f32_dot(piece, hits, TN)
    own_slot = slot_of_row[...] & 31
    line = iota((own_slots, n_rows), 0)
    mine = line == own_slot
    best_ref[...] = jnp.sum(jnp.where(mine, found[:own_slots], 0.0), axis=0, keepdims=True)
    sim_ref[...] = jnp.sum(
        jnp.where(mine, found[own_slots : 2 * own_slots], 0.0), axis=0, keepdims=True
    )
    swap.wait()
    owned_here = (iota((2 * LOCAL, width), 0) // LOCAL) == feat
    cent_ref[...] = jnp.where(owned_here, cent_mine[feat], cent_other[...]).astype(jnp.bfloat16)

    for local in range(LOCAL):
        sent = send.at[local, pl.ds(0, DEVICES - 1)]
        pltpu.make_async_copy(sent, sent, send_sem.at[local]).wait()
    sent = meta_send.at[pl.ds(0, SOURCES - 1)]
    pltpu.make_async_copy(sent, sent, meta_send_sem).wait()
    sent = back_recv.at[pl.ds(0, DEVICES - 1)]
    pltpu.make_async_copy(sent, sent, back_send_sem).wait()


def body(embeddings, assignments, order_index, cluster_blocks):
    n_rows, width = embeddings.shape
    members = SOURCES * SLOTS
    vmem = pl.BlockSpec(memory_space=pltpu.VMEM)
    dma = pltpu.SemaphoreType.DMA
    centroids, sims, bests = pl.pallas_call(
        kernel,
        out_shape=(
            jax.ShapeDtypeStruct((2 * LOCAL, width), jnp.bfloat16),
            jax.ShapeDtypeStruct((1, n_rows), jnp.float32),
            jax.ShapeDtypeStruct((1, n_rows), jnp.float32),
        ),
        in_specs=[pl.BlockSpec(memory_space=pl.ANY), vmem, vmem],
        out_specs=(vmem, vmem, vmem),
        scratch_shapes=[
            pltpu.VMEM((n_rows, width), jnp.bfloat16),
            pltpu.VMEM((1, n_rows), jnp.int32),
            pltpu.VMEM((DEVICES, n_rows), jnp.bfloat16),
            pltpu.VMEM((LOCAL, DEVICES, SLOTS, width), jnp.bfloat16),
            pltpu.VMEM((LOCAL, 2, SOURCES, SLOTS, width), jnp.bfloat16),
            pltpu.VMEM((DEVICES, 1, DEVICES), jnp.float32),
            pltpu.VMEM((SOURCES, 1, DEVICES), jnp.float32),
            pltpu.VMEM((LOCAL, members, 1), jnp.float32),
            pltpu.VMEM((LOCAL, 1, members), jnp.float32),
            pltpu.VMEM((2, 2 * LOCAL, width), jnp.float32),
            pltpu.VMEM((2 * LOCAL, width), jnp.float32),
            pltpu.VMEM((SOURCES, 1, DEVICES), jnp.float32),
            pltpu.VMEM((DEVICES, 1, DEVICES), jnp.float32),
            dma(()),
            dma((LOCAL,)),
            dma((LOCAL,)),
            dma(()),
            dma(()),
            dma(()),
            dma(()),
            dma(()),
            dma(()),
        ],
        compiler_params=pltpu.CompilerParams(
            collective_id=0, has_side_effects=True, vmem_limit_bytes=56 * 2**20
        ),
        name="dedup_window",
    )(embeddings, assignments.reshape(1, n_rows), order_index.reshape(1, n_rows))
    return centroids, sims.reshape(n_rows), bests.reshape(n_rows)


def solution(mesh):
    return jax.shard_map(
        body,
        mesh=mesh,
        in_specs=(P("dp", "feat"), P("dp"), P("dp"), P()),
        out_specs=(P("dp", "feat"), P("dp"), P("dp")),
        check_vma=False,
    )
```

time: 1080 us -> 90.3 us (0.08)
  waiting for transfers between devices: 727 us -> 0 us
  blocking collectives: 174 us -> 0 us
  Pallas kernels: 0 us -> 85.4 us
  matrix products: 62.4 us -> 0 us
  starting transfers between devices: 31.3 us -> 0 us
  local copies, waits for them, and re-layouts: 34.7 us -> 3.89 us
  other arithmetic: 25.2 us -> 0 us
  between operations: 13.9 us -> 0.64 us
    psum x1 -> x0, waiting for transfers between devices: 468 us -> none  [body(): total_sums, total_counts = lax.psum((partial_sums, partial_counts), 'dp')]
    all_gather x8 -> x0, waiting for transfers between devices: 197 us -> none  [visit(): full_rows = lax.all_gather(slice_rows, 'feat', axis=1, tiled=True)]
    psum x3 -> x0, blocking collectives: 174 us -> none  [the longest x1 165 us: body(): total_sums, total_counts = lax.psum((partial_sums, partial_counts), 'dp')]
    pallas_call x0 -> x1, Pallas kernels: none -> 85.4 us  [body(): pl.pallas_call(kernel, out_shape=(jax.ShapeDtypeStruct((2 * LOCAL, width)...]
    dot_general x16 -> x0, matrix products: 62.4 us -> none  [the longest x4 35.5 us: place_block(): jnp.dot(hits.astype(jnp.bfloat16), rows_piece, preferred_element_type=jnp...]
    all_to_all x3 -> x0, waiting for transfers between devices: 62.1 us -> none  [the longest x1 50.1 us: body(): lax.all_to_all(send_rows.reshape(n_owners, cl_local * per_source, local_w...]
    all_to_all x3 -> x0, starting transfers between devices: 31 us -> none  [the longest x1 12.7 us: body(): lax.all_to_all(send_order.reshape(n_owners, cl_local * per_source), 'dp',...]
    dynamic_slice x35 -> x0, local copies, waits for them, and re-layouts: 27.3 us -> none  [the longest x8 15.1 us: visit(): lax.dynamic_index_in_dim(packed, cluster_index, 0, keepdims=False)]
  transfers between devices with their start and end apart: 12 -> 0, of which waited for: 12 -> 0; matrix products, arithmetic and copies ran while one was open for 2% -> 0% of each run, Pallas kernels for 0% -> 0%
where the time goes in v1:
time: 90.3 us; the launch traced here: 89.9 us
  Pallas kernels  85.4 us (95%)
  local copies, waits for them, and re-layouts  3.89 us (4%)
    pallas_call x1, Pallas kernels, body(): pl.pallas_call(kernel, out_shape=(jax.ShapeDtypeStruct((2 * LOCAL, width)...  85.4 us
    unnamed x3, local copies, waits for them, and re-layouts  3.89 us

profile of v1, /device:TPU:1, one launch (start us, length us, event | category | flops | bytes accessed | tf_op | source)
XLA Modules:
  0.0 89.9 jit_solution(2692293639542366676)
XLA Ops:
  0.6 85.4 %dedup_window.1 = (bf16[8,512]{1,0:T(8,128)(2,1)}, f32[1,2048]{1,0:T(1,128)}, f32[1,2048]{1,0:T(1,128)}) custom-call(bf16[2048,512]{1,0:T(8,128)(2,1)} %rows_hbm.1, s32[1,2048]{1,0:T(1,128)} %bitcast.4, s32[1,2048]{1,0:T(1,128)} %bitcast.5), custom_call_target="tpu_custom_call" | custom-call | tf_op jit(solution)/shard_map/dedup_window/pallas_call | solution.py:320
  86.0 1.3 %copy.9 = bf16[8,512]{1,0:T(8,128)(2,1)} copy(bf16[8,512]{1,0:T(8,128)(2,1)} %get-tuple-element.12) | data formatting | bytes 16384
  87.3 1.3 %copy.10 = f32[2048]{0:T(1024)} copy(f32[2048]{0:T(1024)} %bitcast.7) | data formatting | bytes 16384
  88.6 1.3 %copy.11 = f32[2048]{0:T(1024)} copy(f32[2048]{0:T(1024)} %bitcast.6) | data formatting | bytes 16384

commit v2 on v1

--- a/solution.py
+++ b/solution.py
@@ -30,13 +30,25 @@
     return dp, feat, (dp // 16, (dp // 4) % 4, (dp // 2) % 2 * 2 + feat, dp % 2)
 
 
-def shifted(place, k):
+def each_device(place, visit, groups=(0, 8)):
     z, y, x, core = place
-    tz = (z + k % 4) % 4
-    ty = (y + (k // 4) % 4) % 4
-    tx = (x + (k // 16) % 4) % 4
-    tc = (core + k // 64) % 2
-    return ((tz * 4 + ty) * 2 + tx // 2) * 2 + tc, tx % 2
+    planes = [(z + d) % 4 * 16 for d in range(4)]
+    lines = [(y + d) % 4 * 4 for d in range(4)]
+    corners = [planes[i % 4] + lines[i // 4] for i in range(16)]
+
+    def column(group, carry):
+        tx = (x + group % 4) % 4
+        tc = (core + group // 4) % 2
+        inner = tx // 2 * 2 + tc
+        for i in range(1 if isinstance(group, int) and group == 0 else 0, 16):
+            visit(group * 16 + i, corners[i] + inner, tx % 2)
+        return carry
+
+    first, last = groups
+    if isinstance(first, int) and first == 0:
+        column(0, 0)
+        first = 1
+    lax.fori_loop(first, last, column, 0)
 
 
 def shifted_owner(place, k):
@@ -103,12 +115,10 @@
 
     barrier = pltpu.get_barrier_semaphore()
 
-    def greet(k, carry):
-        tdp, tfeat = shifted(place, k)
+    def greet(k, tdp, tfeat):
         pl.semaphore_signal(barrier, inc=1, device_id=(tdp, tfeat), device_id_type=MESH)
-        return carry
-
-    lax.fori_loop(1, DEVICES, greet, 0)
+
+    each_device(place, greet)
 
     part = 256
     n_clusters = DEVICES * LOCAL
@@ -141,33 +151,7 @@
     meta = f32_dot(hits_owner[...], digits.astype(jnp.bfloat16), NT)
     meta_send[:, 0, :] = meta
 
-    load.wait()
-    pl.semaphore_wait(barrier, DEVICES - 1)
-
-    def meta_out(k, carry):
-        tdp, tfeat = shifted(place, k)
-
-        @pl.when(tfeat == feat)
-        def _():
-            pltpu.make_async_remote_copy(
-                meta_send.at[tdp * 2 + feat],
-                meta_recv.at[dp],
-                meta_send_sem,
-                meta_recv_sem,
-                device_id=(tdp, feat),
-                device_id_type=MESH,
-            ).start()
-
-        return carry
-
-    lax.fori_loop(1, DEVICES, meta_out, 0)
-    pltpu.make_async_copy(meta_send.at[dp * 2 + feat], meta_recv.at[dp], meta_recv_sem).start()
-
-    n_chunks = DEVICES // CHUNK
-
-    def pack(step, carry):
-        local = step // n_chunks
-        chunk = step % n_chunks
+    def pack(local, chunk):
         q = iota((CHUNK * SLOTS, 1), 0)
         owner = shifted_owner(place, chunk * CHUNK + (q >> 3))
         wanted = owner * own_slots + local * SLOTS + (q & 7)
@@ -177,9 +161,8 @@
             jnp.bfloat16
         )
 
-        def ship(i, carry):
-            k = chunk * CHUNK + i
-            tdp, tfeat = shifted(place, k)
+    def ship_to(local):
+        def ship(k, tdp, tfeat):
             pltpu.make_async_remote_copy(
                 send.at[local, k],
                 recv.at[local, feat, dp],
@@ -188,22 +171,68 @@
                 device_id=(tdp, tfeat),
                 device_id_type=MESH,
             ).start()
+
+        return ship
+
+    def keep(local):
+        pltpu.make_async_copy(
+            send.at[local, 0], recv.at[local, feat, dp], recv_sem.at[local]
+        ).start()
+
+    n_chunks = DEVICES // CHUNK
+    chunk_groups = CHUNK // 16
+
+    def pack_first(chunk, carry):
+        pack(0, chunk)
+        return carry
+
+    load.wait()
+    lax.fori_loop(0, n_chunks, pack_first, 0)
+    pl.semaphore_wait(barrier, DEVICES - 1)
+    each_device(place, ship_to(0))
+    keep(0)
+
+    z, y, x, core = place
+
+    def meta_out(group, carry):
+        tz = (z + group // 4) % 4
+        ty = (y + group % 4) % 4
+        for i in range(4):
+            tdp = ((tz * 4 + ty) * 2 + (x // 2 + i // 2) % 2) * 2 + (core + i) % 2
+
+            def start():
+                pltpu.make_async_remote_copy(
+                    meta_send.at[tdp * 2 + feat],
+                    meta_recv.at[dp],
+                    meta_send_sem,
+                    meta_recv_sem,
+                    device_id=(tdp, feat),
+                    device_id_type=MESH,
+                ).start()
+
+            if i == 0:
+                pl.when(group > 0)(start)
+            else:
+                start()
+        return carry
+
+    lax.fori_loop(0, 16, meta_out, 0)
+    pltpu.make_async_copy(meta_send.at[dp * 2 + feat], meta_recv.at[dp], meta_recv_sem).start()
+
+    def phase(local, carry):
+        pack(local, 0)
+        each_device(place, ship_to(local), (0, chunk_groups))
+        keep(local)
+
+        def more(chunk, carry):
+            pack(local, chunk)
+            each_device(place, ship_to(local), (chunk * chunk_groups, (chunk + 1) * chunk_groups))
             return carry
 
-        @pl.when(chunk == 0)
-        def _():
-            pltpu.make_async_copy(
-                send.at[local, 0], recv.at[local, feat, dp], recv_sem.at[local]
-            ).start()
-            lax.fori_loop(1, CHUNK, ship, 0)
-
-        @pl.when(chunk > 0)
-        def _():
-            lax.fori_loop(0, CHUNK, ship, 0)
-
+        lax.fori_loop(1, n_chunks, more, 0)
         return carry
 
-    lax.fori_loop(0, LOCAL * n_chunks, pack, 0)
+    lax.fori_loop(1, LOCAL, phase, 0)
 
     pltpu.make_async_copy(meta_recv, meta_recv, meta_recv_sem).wait()
     meta_in = meta_recv[:, 0, :].astype(jnp.bfloat16)
@@ -270,8 +299,7 @@
         device_id_type=MESH,
     )
 
-    def back_out(k, carry):
-        tdp, tfeat = shifted(place, k)
+    def back_out(k, tdp, tfeat):
         pltpu.make_async_remote_copy(
             back_send.at[tdp],
             back_recv.at[dp * 2 + feat],
@@ -280,9 +308,8 @@
             device_id=(tdp, tfeat),
             device_id_type=MESH,
         ).start()
-        return carry
-
-    lax.fori_loop(1, DEVICES, back_out, 0)
+
+    each_device(place, back_out)
     pltpu.make_async_copy(back_send.at[dp], back_recv.at[dp * 2 + feat], back_recv_sem).start()
     swap.start()
 

time: 90.3 us -> 79.5 us (0.88)
  Pallas kernels: 85.4 us -> 74.5 us
    pallas_call x1, Pallas kernels: 85.4 us -> 74.5 us  [body(): pl.pallas_call(kernel, out_shape=(jax.ShapeDtypeStruct((2 * LOCAL, width)...]
where the time goes in v2:
time: 79.5 us; the launch traced here: 79 us
  Pallas kernels  74.5 us (94%)
  local copies, waits for them, and re-layouts  3.89 us (5%)
    pallas_call x1, Pallas kernels, body(): pl.pallas_call(kernel, out_shape=(jax.ShapeDtypeStruct((2 * LOCAL, width)...  74.5 us
    unnamed x3, local copies, waits for them, and re-layouts  3.89 us

profile of v2, /device:TPU:1, one launch (start us, length us, event | category | flops | bytes accessed | tf_op | source)
XLA Modules:
  0.0 79.0 jit_solution(8580781225843847291)
XLA Ops:
  0.6 74.5 %dedup_window.1 = (bf16[8,512]{1,0:T(8,128)(2,1)}, f32[1,2048]{1,0:T(1,128)}, f32[1,2048]{1,0:T(1,128)}) custom-call(bf16[2048,512]{1,0:T(8,128)(2,1)} %rows_hbm.1, s32[1,2048]{1,0:T(1,128)} %bitcast.4, s32[1,2048]{1,0:T(1,128)} %bitcast.5), custom_call_target="tpu_custom_call" | custom-call | tf_op jit(solution)/shard_map/dedup_window/pallas_call | solution.py:347
  75.1 1.3 %copy.9 = bf16[8,512]{1,0:T(8,128)(2,1)} copy(bf16[8,512]{1,0:T(8,128)(2,1)} %get-tuple-element.12) | data formatting | bytes 16384
  76.4 1.3 %copy.10 = f32[2048]{0:T(1024)} copy(f32[2048]{0:T(1024)} %bitcast.7) | data formatting | bytes 16384
  77.7 1.3 %copy.11 = f32[2048]{0:T(1024)} copy(f32[2048]{0:T(1024)} %bitcast.6) | data formatting | bytes 16384

commit v3 on v2

--- a/solution.py
+++ b/solution.py
@@ -30,33 +30,43 @@
     return dp, feat, (dp // 16, (dp // 4) % 4, (dp // 2) % 2 * 2 + feat, dp % 2)
 
 
+def far_first(a):
+    return (2 - a + a // 2 * 3 + a // 3 * 2) % 4
+
+
 def each_device(place, visit, groups=(0, 8)):
     z, y, x, core = place
-    planes = [(z + d) % 4 * 16 for d in range(4)]
-    lines = [(y + d) % 4 * 4 for d in range(4)]
+    planes = [(z + far_first(d)) % 4 * 16 for d in range(4)]
+    lines = [(y + far_first(d)) % 4 * 4 for d in range(4)]
     corners = [planes[i % 4] + lines[i // 4] for i in range(16)]
 
     def column(group, carry):
-        tx = (x + group % 4) % 4
-        tc = (core + group // 4) % 2
+        tx = (x + far_first(group % 4)) % 4
+        tc = (core + 1 - group // 4) % 2
         inner = tx // 2 * 2 + tc
-        for i in range(1 if isinstance(group, int) and group == 0 else 0, 16):
+        for i in range(15 if isinstance(group, int) else 16):
             visit(group * 16 + i, corners[i] + inner, tx % 2)
         return carry
 
     first, last = groups
-    if isinstance(first, int) and first == 0:
-        column(0, 0)
-        first = 1
-    lax.fori_loop(first, last, column, 0)
-
-
-def shifted_owner(place, k):
+    if isinstance(last, int) and last == 8:
+        if first < 7:
+            lax.fori_loop(first, 7, column, 0)
+        column(7, 0)
+    else:
+        lax.fori_loop(first, last, column, 0)
+
+
+def owner_at(place, k):
     z, y, x, core = place
-    tz = (z + (k & 3)) & 3
-    ty = (y + ((k >> 2) & 3)) & 3
-    tx = (x + ((k >> 4) & 3)) & 3
-    tc = (core + (k >> 6)) & 1
+
+    def shift(a):
+        return 2 - a + (a >> 1) * 3 + ((a + 1) >> 2) * 2
+
+    tz = (z + shift(k & 3)) & 3
+    ty = (y + shift((k >> 2) & 3)) & 3
+    tx = (x + shift((k >> 4) & 3)) & 3
+    tc = (core + 1 - (k >> 6)) & 1
     return (tz << 5) + (ty << 3) + ((tx >> 1) << 2) + (tc << 1) + (tx & 1)
 
 
@@ -78,11 +88,13 @@
 
 def kernel(
     rows_hbm,
-    assign_ref,
-    order_ref,
+    assign_hbm,
+    order_hbm,
     cent_ref,
     sim_ref,
     best_ref,
+    assign_ref,
+    order_ref,
     rows,
     slot_of_row,
     hits_owner,
@@ -96,7 +108,7 @@
     cent_other,
     back_send,
     back_recv,
-    load_sem,
+    load_sems,
     send_sem,
     recv_sem,
     meta_send_sem,
@@ -110,21 +122,25 @@
     n_rows = rows.shape[0]
     width = rows.shape[1]
     members = SOURCES * SLOTS
-    load = pltpu.make_async_copy(rows_hbm, rows, load_sem)
-    load.start()
-
     barrier = pltpu.get_barrier_semaphore()
 
     def greet(k, tdp, tfeat):
         pl.semaphore_signal(barrier, inc=1, device_id=(tdp, tfeat), device_id_type=MESH)
 
     each_device(place, greet)
+    load_assign = pltpu.make_async_copy(assign_hbm, assign_ref, load_sems.at[0])
+    load_order = pltpu.make_async_copy(order_hbm, order_ref, load_sems.at[1])
+    load_rows = pltpu.make_async_copy(rows_hbm, rows, load_sems.at[2])
+    load_assign.start()
+    load_order.start()
+    load_rows.start()
 
     part = 256
     n_clusters = DEVICES * LOCAL
     before = onehot(iota((part, part), 0) < iota((part, part), 1))
     ones = jnp.ones((part, part), jnp.bfloat16)
 
+    load_assign.wait()
     counted = jnp.zeros((n_clusters, part), jnp.float32)
     for block in range(n_rows // part):
         piece = assign_ref[:, block * part : (block + 1) * part]
@@ -139,6 +155,7 @@
     slots = slot_of_row[...]
     own_slots = LOCAL * SLOTS
     hits_owner[...] = onehot(iota((DEVICES, n_rows), 0) == (slots >> 5))
+    load_order.wait()
     orders = order_ref[...]
     line = iota((DEVICES, n_rows), 0)
     kind = line >> 5
@@ -153,7 +170,7 @@
 
     def pack(local, chunk):
         q = iota((CHUNK * SLOTS, 1), 0)
-        owner = shifted_owner(place, chunk * CHUNK + (q >> 3))
+        owner = owner_at(place, chunk * CHUNK + (q >> 3))
         wanted = owner * own_slots + local * SLOTS + (q & 7)
         hits = onehot(wanted == slot_of_row[...])
         packed = jnp.dot(hits, rows[...], preferred_element_type=jnp.float32)
@@ -176,7 +193,7 @@
 
     def keep(local):
         pltpu.make_async_copy(
-            send.at[local, 0], recv.at[local, feat, dp], recv_sem.at[local]
+            send.at[local, DEVICES - 1], recv.at[local, feat, dp], recv_sem.at[local]
         ).start()
 
     n_chunks = DEVICES // CHUNK
@@ -186,7 +203,7 @@
         pack(0, chunk)
         return carry
 
-    load.wait()
+    load_rows.wait()
     lax.fori_loop(0, n_chunks, pack_first, 0)
     pl.semaphore_wait(barrier, DEVICES - 1)
     each_device(place, ship_to(0))
@@ -220,16 +237,15 @@
     pltpu.make_async_copy(meta_send.at[dp * 2 + feat], meta_recv.at[dp], meta_recv_sem).start()
 
     def phase(local, carry):
-        pack(local, 0)
-        each_device(place, ship_to(local), (0, chunk_groups))
-        keep(local)
-
-        def more(chunk, carry):
+        def ahead(chunk, carry):
             pack(local, chunk)
             each_device(place, ship_to(local), (chunk * chunk_groups, (chunk + 1) * chunk_groups))
             return carry
 
-        lax.fori_loop(1, n_chunks, more, 0)
+        lax.fori_loop(0, n_chunks - 1, ahead, 0)
+        pack(local, n_chunks - 1)
+        each_device(place, ship_to(local), (8 - chunk_groups, 8))
+        keep(local)
         return carry
 
     lax.fori_loop(1, LOCAL, phase, 0)
@@ -351,9 +367,11 @@
             jax.ShapeDtypeStruct((1, n_rows), jnp.float32),
             jax.ShapeDtypeStruct((1, n_rows), jnp.float32),
         ),
-        in_specs=[pl.BlockSpec(memory_space=pl.ANY), vmem, vmem],
+        in_specs=[pl.BlockSpec(memory_space=pl.ANY)] * 3,
         out_specs=(vmem, vmem, vmem),
         scratch_shapes=[
+            pltpu.VMEM((1, n_rows), jnp.int32),
+            pltpu.VMEM((1, n_rows), jnp.int32),
             pltpu.VMEM((n_rows, width), jnp.bfloat16),
             pltpu.VMEM((1, n_rows), jnp.int32),
             pltpu.VMEM((DEVICES, n_rows), jnp.bfloat16),
@@ -367,7 +385,7 @@
             pltpu.VMEM((2 * LOCAL, width), jnp.float32),
             pltpu.VMEM((SOURCES, 1, DEVICES), jnp.float32),
             pltpu.VMEM((DEVICES, 1, DEVICES), jnp.float32),
-            dma(()),
+            dma((3,)),
             dma((LOCAL,)),
             dma((LOCAL,)),
             dma(()),

time: 79.5 us -> 76.1 us (0.957)
  Pallas kernels: 74.5 us -> 71.2 us
    pallas_call x1, Pallas kernels: 74.5 us -> 71.2 us  [body(): pl.pallas_call(kernel, out_shape=(jax.ShapeDtypeStruct((2 * LOCAL, width)...]
where the time goes in v3:
time: 76.1 us; the launch traced here: 75.8 us
  Pallas kernels  71.2 us (94%)
  local copies, waits for them, and re-layouts  3.89 us (5%)
    pallas_call x1, Pallas kernels, body(): pl.pallas_call(kernel, out_shape=(jax.ShapeDtypeStruct((2 * LOCAL, width)...  71.2 us
    unnamed x3, local copies, waits for them, and re-layouts  3.89 us

profile of v3, /device:TPU:1, one launch (start us, length us, event | category | flops | bytes accessed | tf_op | source)
XLA Modules:
  0.0 75.8 jit_solution(17800702999941128442)
XLA Ops:
  0.6 71.2 %dedup_window.1 = (bf16[8,512]{1,0:T(8,128)(2,1)}, f32[1,2048]{1,0:T(1,128)}, f32[1,2048]{1,0:T(1,128)}) custom-call(bf16[2048,512]{1,0:T(8,128)(2,1)} %rows_hbm.1, s32[1,2048]{1,0:T(1,128)} %bitcast.4, s32[1,2048]{1,0:T(1,128)} %bitcast.5), custom_call_target="tpu_custom_call" | custom-call | tf_op jit(solution)/shard_map/dedup_window/pallas_call | solution.py:363
  71.9 1.3 %copy.9 = bf16[8,512]{1,0:T(8,128)(2,1)} copy(bf16[8,512]{1,0:T(8,128)(2,1)} %get-tuple-element.12) | data formatting | bytes 16384
  73.2 1.3 %copy.10 = f32[2048]{0:T(1024)} copy(f32[2048]{0:T(1024)} %bitcast.7) | data formatting | bytes 16384
  74.5 1.3 %copy.11 = f32[2048]{0:T(1024)} copy(f32[2048]{0:T(1024)} %bitcast.6) | data formatting | bytes 16384

commit v4 on v3

--- a/solution.py
+++ b/solution.py
@@ -152,8 +152,60 @@
         if block + 1 < n_rows // part:
             counted = counted + jnp.dot(member_b, ones, preferred_element_type=jnp.float32)
 
+    own_slots = LOCAL * SLOTS
+
+    def pack(local, chunk):
+        q = iota((CHUNK * SLOTS, 1), 0)
+        owner = owner_at(place, chunk * CHUNK + (q >> 3))
+        wanted = owner * own_slots + local * SLOTS + (q & 7)
+        hits = onehot(wanted == slot_of_row[...])
+        packed = jnp.dot(hits, rows[...], preferred_element_type=jnp.float32)
+        send[local, pl.ds(chunk * CHUNK, CHUNK)] = packed.reshape(CHUNK, SLOTS, width).astype(
+            jnp.bfloat16
+        )
+
+    def ship_to(local):
+        def ship(k, tdp, tfeat):
+            pltpu.make_async_remote_copy(
+                send.at[local, k],
+                recv.at[local, feat, dp],
+                send_sem.at[local],
+                recv_sem.at[local],
+                device_id=(tdp, tfeat),
+                device_id_type=MESH,
+            ).start()
+
+        return ship
+
+    def keep(local):
+        pltpu.make_async_copy(
+            send.at[local, DEVICES - 1], recv.at[local, feat, dp], recv_sem.at[local]
+        ).start()
+
+    n_chunks = DEVICES // CHUNK
+    chunk_groups = CHUNK // 16
+
+    def ahead_of(local):
+        def ahead(chunk, carry):
+            pack(local, chunk)
+            each_device(place, ship_to(local), (chunk * chunk_groups, (chunk + 1) * chunk_groups))
+            return carry
+
+        return ahead
+
+    def finish(local):
+        pack(local, n_chunks - 1)
+        each_device(place, ship_to(local), (8 - chunk_groups, 8))
+        keep(local)
+
+    load_rows.wait()
+    pack(0, 0)
+    pl.semaphore_wait(barrier, DEVICES - 1)
+    each_device(place, ship_to(0), (0, chunk_groups))
+    lax.fori_loop(1, n_chunks - 1, ahead_of(0), 0)
+    finish(0)
+
     slots = slot_of_row[...]
-    own_slots = LOCAL * SLOTS
     hits_owner[...] = onehot(iota((DEVICES, n_rows), 0) == (slots >> 5))
     load_order.wait()
     orders = order_ref[...]
@@ -168,47 +220,6 @@
     meta = f32_dot(hits_owner[...], digits.astype(jnp.bfloat16), NT)
     meta_send[:, 0, :] = meta
 
-    def pack(local, chunk):
-        q = iota((CHUNK * SLOTS, 1), 0)
-        owner = owner_at(place, chunk * CHUNK + (q >> 3))
-        wanted = owner * own_slots + local * SLOTS + (q & 7)
-        hits = onehot(wanted == slot_of_row[...])
-        packed = jnp.dot(hits, rows[...], preferred_element_type=jnp.float32)
-        send[local, pl.ds(chunk * CHUNK, CHUNK)] = packed.reshape(CHUNK, SLOTS, width).astype(
-            jnp.bfloat16
-        )
-
-    def ship_to(local):
-        def ship(k, tdp, tfeat):
-            pltpu.make_async_remote_copy(
-                send.at[local, k],
-                recv.at[local, feat, dp],
-                send_sem.at[local],
-                recv_sem.at[local],
-                device_id=(tdp, tfeat),
-                device_id_type=MESH,
-            ).start()
-
-        return ship
-
-    def keep(local):
-        pltpu.make_async_copy(
-            send.at[local, DEVICES - 1], recv.at[local, feat, dp], recv_sem.at[local]
-        ).start()
-
-    n_chunks = DEVICES // CHUNK
-    chunk_groups = CHUNK // 16
-
-    def pack_first(chunk, carry):
-        pack(0, chunk)
-        return carry
-
-    load_rows.wait()
-    lax.fori_loop(0, n_chunks, pack_first, 0)
-    pl.semaphore_wait(barrier, DEVICES - 1)
-    each_device(place, ship_to(0))
-    keep(0)
-
     z, y, x, core = place
 
     def meta_out(group, carry):
@@ -237,15 +248,8 @@
     pltpu.make_async_copy(meta_send.at[dp * 2 + feat], meta_recv.at[dp], meta_recv_sem).start()
 
     def phase(local, carry):
-        def ahead(chunk, carry):
-            pack(local, chunk)
-            each_device(place, ship_to(local), (chunk * chunk_groups, (chunk + 1) * chunk_groups))
-            return carry
-
-        lax.fori_loop(0, n_chunks - 1, ahead, 0)
-        pack(local, n_chunks - 1)
-        each_device(place, ship_to(local), (8 - chunk_groups, 8))
-        keep(local)
+        lax.fori_loop(0, n_chunks - 1, ahead_of(local), 0)
+        finish(local)
         return carry
 
     lax.fori_loop(1, LOCAL, phase, 0)
@@ -355,6 +359,11 @@
     pltpu.make_async_copy(sent, sent, back_send_sem).wait()
 
 
+def hand_over(*refs):
+    for source, target in zip(refs[:3], refs[3:]):
+        target[...] = source[...]
+
+
 def body(embeddings, assignments, order_index, cluster_blocks):
     n_rows, width = embeddings.shape
     members = SOURCES * SLOTS
@@ -400,6 +409,10 @@
         ),
         name="dedup_window",
     )(embeddings, assignments.reshape(1, n_rows), order_index.reshape(1, n_rows))
+    outs = tuple(jax.ShapeDtypeStruct(x.shape, x.dtype) for x in (centroids, sims, bests))
+    centroids, sims, bests = pl.pallas_call(
+        hand_over, out_shape=outs, in_specs=[vmem] * 3, out_specs=(vmem,) * 3, name="hand_over"
+    )(centroids, sims, bests)
     return centroids, sims.reshape(n_rows), bests.reshape(n_rows)
 
 

time: 76.1 us -> 70.6 us (0.928)
  local copies, waits for them, and re-layouts: 3.89 us -> 0 us
  Pallas kernels: 71.2 us -> 69.8 us
    unnamed x3 -> x0, local copies, waits for them, and re-layouts: 3.89 us -> none
    pallas_call x1, Pallas kernels: 71.2 us -> 68.5 us  [body(): pl.pallas_call(kernel, out_shape=(jax.ShapeDtypeStruct((2 * LOCAL, width)...]
    pallas_call x0 -> x1, Pallas kernels: none -> 1.34 us  [body(): pl.pallas_call(hand_over, out_shape=outs, in_specs=[vmem] * 3, out_specs=...]
where the time goes in v4:
time: 70.6 us; the launch traced here: 70.4 us
  Pallas kernels  69.8 us (99%)
    pallas_call x1, Pallas kernels, body(): pl.pallas_call(kernel, out_shape=(jax.ShapeDtypeStruct((2 * LOCAL, width)...  68.5 us

profile of v4, /device:TPU:1, one launch (start us, length us, event | category | flops | bytes accessed | tf_op | source)
XLA Modules:
  0.0 70.4 jit_solution(11832581864249256174)
XLA Ops:
  0.6 68.5 %dedup_window.1 = (bf16[8,512]{1,0:T(8,128)(2,1)}, f32[1,2048]{1,0:T(1,128)}, f32[1,2048]{1,0:T(1,128)}) custom-call(bf16[2048,512]{1,0:T(8,128)(2,1)} %rows_hbm.1, s32[1,2048]{1,0:T(1,128)} %bitcast.4, s32[1,2048]{1,0:T(1,128)} %bitcast.5), custom_call_target="tpu_custom_call" | custom-call | tf_op jit(solution)/shard_map/dedup_window/pallas_call | solution.py:372
  69.1 1.3 %hand_over.1 = (bf16[8,512]{1,0:T(8,128)(2,1)}, f32[1,2048]{1,0:T(1,128)}, f32[1,2048]{1,0:T(1,128)}) custom-call(bf16[8,512]{1,0:T(8,128)(2,1)} %get-tuple-element.9.refs_0_, f32[1,2048]{1,0:T(1,128)} %get-tuple-element.10.refs_1_, f32[1,2048]{1,0:T(1,128)} %get-tuple-element.11.refs_2_), custom_call_target="tpu_custom_call" | custom-call | tf_op jit(solution)/shard_map/hand_over/pallas_call | solution.py:413

commit v5 on v4

--- a/solution.py
+++ b/solution.py
@@ -34,7 +34,7 @@
     return (2 - a + a // 2 * 3 + a // 3 * 2) % 4
 
 
-def each_device(place, visit, groups=(0, 8)):
+def each_device(place, visit, groups=(0, 8), unrolled=False):
     z, y, x, core = place
     planes = [(z + far_first(d)) % 4 * 16 for d in range(4)]
     lines = [(y + far_first(d)) % 4 * 4 for d in range(4)]
@@ -44,10 +44,14 @@
         tx = (x + far_first(group % 4)) % 4
         tc = (core + 1 - group // 4) % 2
         inner = tx // 2 * 2 + tc
-        for i in range(15 if isinstance(group, int) else 16):
+        for i in range(15 if isinstance(group, int) and group == 7 else 16):
             visit(group * 16 + i, corners[i] + inner, tx % 2)
         return carry
 
+    if unrolled:
+        for group in range(*groups):
+            column(group, 0)
+        return
     first, last = groups
     if isinstance(last, int) and last == 8:
         if first < 7:
@@ -127,7 +131,7 @@
     def greet(k, tdp, tfeat):
         pl.semaphore_signal(barrier, inc=1, device_id=(tdp, tfeat), device_id_type=MESH)
 
-    each_device(place, greet)
+    each_device(place, greet, unrolled=True)
     load_assign = pltpu.make_async_copy(assign_hbm, assign_ref, load_sems.at[0])
     load_order = pltpu.make_async_copy(order_hbm, order_ref, load_sems.at[1])
     load_rows = pltpu.make_async_copy(rows_hbm, rows, load_sems.at[2])
@@ -275,8 +279,7 @@
 
     lane = iota((members, DEVICES), 1)
     slot_of_member = iota((members, DEVICES), 0) & 7
-    back = jnp.zeros((SOURCES, DEVICES), jnp.float32)
-    for local in range(LOCAL):
+    def own(local, back):
         pltpu.make_async_copy(recv.at[local], recv.at[local], recv_sem.at[local]).wait()
         values = jnp.concatenate(
             [recv[local, h].astype(jnp.float32).reshape(members, width) for h in range(2)], axis=1
@@ -290,9 +293,7 @@
         norm = jnp.sum(averages * averages, axis=1, keepdims=True)
         centroid = (averages / jnp.sqrt(norm + epsilon)).astype(jnp.bfloat16).astype(jnp.float32)
         for h in range(2):
-            half = centroid[:, h * width : (h + 1) * width]
-            cent_mine[h, local : local + 1] = half
-            cent_mine[h, local + LOCAL : local + LOCAL + 1] = half
+            cent_mine[h, local] = centroid[:, h * width : (h + 1) * width]
         products = jnp.sum(values * centroid, axis=1, keepdims=True)
         inverse = 1.0 / lengths
         sim = products * inverse
@@ -308,7 +309,9 @@
             back = back + jnp.dot(piece, to_lane, preferred_element_type=jnp.float32)
         for piece in thirds(sim_lanes):
             back = back + jnp.dot(of_source, piece, preferred_element_type=jnp.float32)
-
+        return back
+
+    back = lax.fori_loop(0, LOCAL, own, jnp.zeros((SOURCES, DEVICES), jnp.float32))
     back_send[:, 0, :] = back
     swap = pltpu.make_async_remote_copy(
         cent_mine.at[1 - feat],
@@ -329,14 +332,14 @@
             device_id_type=MESH,
         ).start()
 
-    each_device(place, back_out)
+    each_device(place, back_out, unrolled=True)
     pltpu.make_async_copy(back_send.at[dp], back_recv.at[dp * 2 + feat], back_recv_sem).start()
     swap.start()
 
     pltpu.make_async_copy(back_recv, back_recv, back_recv_sem).wait()
-    table = back_recv[:, 0, :]
+    table = back_recv[:, 0, :][:, : 2 * own_slots]
     hits = hits_owner[...]
-    found = jnp.zeros((DEVICES, n_rows), jnp.float32)
+    found = jnp.zeros((2 * own_slots, n_rows), jnp.float32)
     for piece in thirds(table):
         found = found + f32_dot(piece, hits, TN)
     own_slot = slot_of_row[...] & 31
@@ -347,8 +350,12 @@
         jnp.where(mine, found[own_slots : 2 * own_slots], 0.0), axis=0, keepdims=True
     )
     swap.wait()
+    mine = [cent_mine[feat, local] for local in range(LOCAL)]
+    other = [cent_other[local] for local in range(LOCAL)]
     owned_here = (iota((2 * LOCAL, width), 0) // LOCAL) == feat
-    cent_ref[...] = jnp.where(owned_here, cent_mine[feat], cent_other[...]).astype(jnp.bfloat16)
+    cent_ref[...] = jnp.where(
+        owned_here, jnp.concatenate(mine + mine), jnp.concatenate(other + other)
+    ).astype(jnp.bfloat16)
 
     for local in range(LOCAL):
         sent = send.at[local, pl.ds(0, DEVICES - 1)]
@@ -390,8 +397,8 @@
             pltpu.VMEM((SOURCES, 1, DEVICES), jnp.float32),
             pltpu.VMEM((LOCAL, members, 1), jnp.float32),
             pltpu.VMEM((LOCAL, 1, members), jnp.float32),
-            pltpu.VMEM((2, 2 * LOCAL, width), jnp.float32),
-            pltpu.VMEM((2 * LOCAL, width), jnp.float32),
+            pltpu.VMEM((2, LOCAL, 1, width), jnp.float32),
+            pltpu.VMEM((LOCAL, 1, width), jnp.float32),
             pltpu.VMEM((SOURCES, 1, DEVICES), jnp.float32),
             pltpu.VMEM((DEVICES, 1, DEVICES), jnp.float32),
             dma((3,)),
@@ -405,13 +412,13 @@
             dma(()),
         ],
         compiler_params=pltpu.CompilerParams(
-            collective_id=0, has_side_effects=True, vmem_limit_bytes=56 * 2**20
+            collective_id=0, has_side_effects=True, vmem_limit_bytes=32 * 2**20
         ),
         name="dedup_window",
-    )(embeddings, assignments.reshape(1, n_rows), order_index.reshape(1, n_rows))
+    )(*[pltpu.with_memory_space_constraint(x, pltpu.HBM) for x in (embeddings, assignments.reshape(1, n_rows), order_index.reshape(1, n_rows))])
     outs = tuple(jax.ShapeDtypeStruct(x.shape, x.dtype) for x in (centroids, sims, bests))
     centroids, sims, bests = pl.pallas_call(
-        hand_over, out_shape=outs, in_specs=[vmem] * 3, out_specs=(vmem,) * 3, name="hand_over"
+        hand_over, out_shape=outs, in_specs=[vmem] * 3, out_specs=(vmem,) * 3, compiler_params=pltpu.CompilerParams(vmem_limit_bytes=2**20), name="hand_over"
     )(centroids, sims, bests)
     return centroids, sims.reshape(n_rows), bests.reshape(n_rows)
 

time: 70.6 us -> 68.8 us (0.975)
  Pallas kernels: 69.8 us -> 68.1 us
    pallas_call x1, Pallas kernels: 68.5 us -> 67.4 us  [body(): pl.pallas_call(kernel, out_shape=(jax.ShapeDtypeStruct((2 * LOCAL, width)...]
    pallas_call x1, Pallas kernels: 1.34 us -> 0.61 us  [body(): pl.pallas_call(hand_over, out_shape=outs, in_specs=[vmem] * 3, out_specs=...]
where the time goes in v5:
time: 68.8 us; the launch traced here: 68.7 us
  Pallas kernels  68.1 us (99%)
    pallas_call x1, Pallas kernels, body(): pl.pallas_call(kernel, out_shape=(jax.ShapeDtypeStruct((2 * LOCAL, width)...  67.4 us

profile of v5, /device:TPU:1, one launch (start us, length us, event | category | flops | bytes accessed | tf_op | source)
XLA Modules:
  0.0 68.7 jit_solution(14835341548996241312)
XLA Ops:
  0.6 67.4 %dedup_window.1 = (bf16[8,512]{1,0:T(8,128)(2,1)S(1)}, f32[1,2048]{1,0:T(1,128)S(1)}, f32[1,2048]{1,0:T(1,128)S(1)}) custom-call(bf16[2048,512]{1,0:T(8,128)(2,1)} %rows_hbm.1, s32[1,2048]{1,0:T(1,128)} %bitcast.4, s32[1,2048]{1,0:T(1,128)} %bitcast.5), custom_call_target="tpu_custom_call" | custom-call | tf_op jit(solution)/shard_map/dedup_window/pallas_call | solution.py:379
  68.1 0.6 hand_over.1

commit v6 on v5

--- a/solution.py
+++ b/solution.py
@@ -305,10 +305,9 @@
         )
         to_lane = onehot(lane == local * SLOTS + slot_of_member)
         sim_lanes = jnp.where(lane == (LOCAL + local) * SLOTS + slot_of_member, sim, 0.0)
-        for piece in thirds(best_of_source):
-            back = back + jnp.dot(piece, to_lane, preferred_element_type=jnp.float32)
-        for piece in thirds(sim_lanes):
-            back = back + jnp.dot(of_source, piece, preferred_element_type=jnp.float32)
+        left = jnp.concatenate([*thirds(best_of_source), of_source, of_source, of_source], axis=1)
+        right = jnp.concatenate([to_lane, to_lane, to_lane, *thirds(sim_lanes)])
+        back = back + jnp.dot(left, right, preferred_element_type=jnp.float32)
         return back
 
     back = lax.fori_loop(0, LOCAL, own, jnp.zeros((SOURCES, DEVICES), jnp.float32))
@@ -336,6 +335,19 @@
     pltpu.make_async_copy(back_send.at[dp], back_recv.at[dp * 2 + feat], back_recv_sem).start()
     swap.start()
 
+    swap.wait()
+    mine = [cent_mine[feat, local] for local in range(LOCAL)]
+    other = [cent_other[local] for local in range(LOCAL)]
+    owned_here = (iota((2 * LOCAL, width), 0) // LOCAL) == feat
+    cent_ref[...] = jnp.where(
+        owned_here, jnp.concatenate(mine + mine), jnp.concatenate(other + other)
+    ).astype(jnp.bfloat16)
+
+    for local in range(LOCAL):
+        sent = send.at[local, pl.ds(0, DEVICES - 1)]
+        pltpu.make_async_copy(sent, sent, send_sem.at[local]).wait()
+    sent = meta_send.at[pl.ds(0, SOURCES - 1)]
+    pltpu.make_async_copy(sent, sent, meta_send_sem).wait()
     pltpu.make_async_copy(back_recv, back_recv, back_recv_sem).wait()
     table = back_recv[:, 0, :][:, : 2 * own_slots]
     hits = hits_owner[...]
@@ -349,19 +361,7 @@
     sim_ref[...] = jnp.sum(
         jnp.where(mine, found[own_slots : 2 * own_slots], 0.0), axis=0, keepdims=True
     )
-    swap.wait()
-    mine = [cent_mine[feat, local] for local in range(LOCAL)]
-    other = [cent_other[local] for local in range(LOCAL)]
-    owned_here = (iota((2 * LOCAL, width), 0) // LOCAL) == feat
-    cent_ref[...] = jnp.where(
-        owned_here, jnp.concatenate(mine + mine), jnp.concatenate(other + other)
-    ).astype(jnp.bfloat16)
-
-    for local in range(LOCAL):
-        sent = send.at[local, pl.ds(0, DEVICES - 1)]
-        pltpu.make_async_copy(sent, sent, send_sem.at[local]).wait()
-    sent = meta_send.at[pl.ds(0, SOURCES - 1)]
-    pltpu.make_async_copy(sent, sent, meta_send_sem).wait()
+
     sent = back_recv.at[pl.ds(0, DEVICES - 1)]
     pltpu.make_async_copy(sent, sent, back_send_sem).wait()
 

time: 68.8 us -> 68.8 us (level)
  no operation moved by 1% of the time
where the time goes in v6:
time: 68.8 us; the launch traced here: 68.7 us
  Pallas kernels  68 us (99%)
    pallas_call x1, Pallas kernels, body(): pl.pallas_call(kernel, out_shape=(jax.ShapeDtypeStruct((2 * LOCAL, width)...  67.4 us

profile of v6, /device:TPU:1, one launch (start us, length us, event | category | flops | bytes accessed | tf_op | source)
XLA Modules:
  0.0 68.7 jit_solution(4915888182520940675)
XLA Ops:
  0.6 67.4 %dedup_window.1 = (bf16[8,512]{1,0:T(8,128)(2,1)S(1)}, f32[1,2048]{1,0:T(1,128)S(1)}, f32[1,2048]{1,0:T(1,128)S(1)}) custom-call(bf16[2048,512]{1,0:T(8,128)(2,1)} %rows_hbm.1, s32[1,2048]{1,0:T(1,128)} %bitcast.4, s32[1,2048]{1,0:T(1,128)} %bitcast.5), custom_call_target="tpu_custom_call" | custom-call | tf_op jit(solution)/shard_map/dedup_window/pallas_call | solution.py:379
  68.1 0.6 hand_over.1
